TPU v7x, 128 devices: a whole 4x4x4 slice. The times are simulated.
128 devices in a mesh: fsdp: 16 (over x, z), dp: 8 (over y, core).
Axes of the slice: x: 4, y: 4, z: 4, core: 2. Of those that a mesh axis runs over, the one named last changes fastest.
Arguments:
- grad_parts: bfloat16 [8, 16384, 2048], P('dp', 'fsdp'), may hold values from -6 to 6
- old_master: float32 [16384, 2048], P(('fsdp', 'dp')), may hold values from -0.25 to 0.25
- old_mean: bfloat16 [16384, 2048], P(('fsdp', 'dp')), may hold values from -1 to 1
- old_mean_scale: bfloat16 [16384], P(('fsdp', 'dp')), may hold values from 0.049804688 to 0.5
- old_square: bfloat16 [16384, 2048], P(('fsdp', 'dp')), may hold values from 0.049804688 to 1
- old_square_scale: bfloat16 [16384], P(('fsdp', 'dp')), may hold values from 0.29882812 to 3
- old_map: int32 [16384], replicated, may hold values from 0 to 16383, as said below
Outputs:
- weights: bfloat16 [16384, 2048], P('fsdp')
- master: float32 [16384, 2048], P(('fsdp', 'dp'))
- mean_codes: bfloat16 [16384, 2048], P(('fsdp', 'dp'))
- mean_scales: bfloat16 [16384], P(('fsdp', 'dp'))
- square_codes: bfloat16 [16384, 2048], P(('fsdp', 'dp'))
- square_scales: bfloat16 [16384], P(('fsdp', 'dp'))
Inputs may be any that keep to these rules, and one draw needn't show every extreme that they name: old_map is a permutation of the old slots; old slot s lies on device s // 128 counted along fsdp+dp with fsdp major, and block b belongs to new owner b // 128 counted the same way. Every device holds exactly 128 old slots; one device holds at most 2 blocks of one new owner, and every draw has a pair with exactly 2.
All inputs are finite; a program needn't handle non-finite values. Where the computation divides by a largest or mean magnitude, that divisor is 1e-20 or more.
Results may differ from a plain program's by a relative error of at most 0.02.
Values may be sent and summed in bfloat16 or wider, within the bound.
No kernel may reach another device: no remote copies, remote signals or barrier semaphores. Data moves between devices by JAX's collectives and lax.ppermute only.
A program may use at most 64 MiB of HBM per device.

v0:
```python
import jax
import jax.numpy as jnp
from jax import lax
from jax.sharding import PartitionSpec as P


def pair_rank(owners, keyed):
    matching = owners[:, None] == owners[None, :]
    before = keyed[None, :] < keyed[:, None]
    return jnp.sum(jnp.where(matching & before, 1, 0), axis=1).astype(jnp.int32)


def route_bf16(chooser, values):
    flat_values = values.reshape((values.shape[0], -1))
    moved = jnp.dot(chooser.astype(jnp.bfloat16), flat_values, preferred_element_type=jnp.float32)
    return moved.astype(jnp.bfloat16).reshape((chooser.shape[0],) + values.shape[1:])


def route_f32(chooser, values):
    return jnp.dot(
        chooser.astype(jnp.float32),
        values,
        precision=lax.Precision.HIGHEST,
        preferred_element_type=jnp.float32,
    )


def block_peak(values):
    return (jnp.max(values, axis=1) + 1e-06).astype(jnp.bfloat16)


def local(grad_parts, old_master, old_mean, old_mean_scale, old_square, old_square_scale, old_map):
    count_all = lax.axis_size(("fsdp", "dp"))
    block_rows = old_master.shape[0]
    block_len = old_master.shape[1]
    peer_cap = max(2, 2 * block_rows // count_all)
    slot_total = count_all * peer_cap
    self_index = lax.axis_index(("fsdp", "dp"))
    gradient = lax.psum_scatter(
        grad_parts[0].astype(jnp.float32).astype(jnp.bfloat16),
        "dp",
        scatter_dimension=0,
        tiled=True,
    ).astype(jnp.float32)
    total_blocks = old_map.shape[0]
    my_slots = self_index * block_rows + jnp.arange(block_rows, dtype=jnp.int32)
    block_ids = jnp.arange(total_blocks, dtype=jnp.int32)
    held_blocks = jnp.sum(
        jnp.where(old_map[None, :] == my_slots[:, None], block_ids[None, :], 0), axis=1
    )
    target = held_blocks // block_rows
    local_pos = held_blocks % block_rows
    sent_rank = pair_rank(target, local_pos)
    wanted = lax.dynamic_slice_in_dim(old_map, self_index * block_rows, block_rows)
    source = wanted // block_rows
    got_rank = pair_rank(source, jnp.arange(block_rows, dtype=jnp.int32))
    slot_ids = jnp.arange(slot_total, dtype=jnp.int32)
    send_flat = target * peer_cap + sent_rank
    placing = slot_ids[:, None] == send_flat[None, :]
    moment_codes = jnp.stack([old_mean, old_square], axis=1)
    moment_scales = jnp.stack([old_mean_scale, old_square_scale], axis=1)
    code_buffer = route_bf16(placing, moment_codes).reshape((count_all, peer_cap, 2, block_len))
    scale_buffer = route_bf16(placing, moment_scales).reshape((count_all, peer_cap, 2))
    master_buffer = route_f32(placing, old_master).reshape((count_all, peer_cap, block_len))
    code_in, scale_in = (
        lax.all_to_all(code_buffer, ("fsdp", "dp"), split_axis=0, concat_axis=0, tiled=True),
        lax.all_to_all(scale_buffer, ("fsdp", "dp"), split_axis=0, concat_axis=0, tiled=True),
    )
    master_in = lax.all_to_all(
        master_buffer.astype(jnp.bfloat16), ("fsdp", "dp"), split_axis=0, concat_axis=0, tiled=True
    ).astype(master_buffer.dtype)
    recv_flat = source * peer_cap + got_rank
    picking = recv_flat[:, None] == slot_ids[None, :]
    code_rows = route_bf16(picking, code_in.reshape((slot_total, 2, block_len))).astype(jnp.float32)
    scale_rows = route_bf16(picking, scale_in.reshape((slot_total, 2))).astype(jnp.float32)
    weight_old = route_f32(picking, master_in.reshape((slot_total, block_len)))
    mean_old = code_rows[:, 0] * scale_rows[:, 0:1]
    square_old = code_rows[:, 1] * scale_rows[:, 1:2]
    mean_next = 0.9 * mean_old + 0.1 * gradient
    square_next = 0.95 * square_old + 0.05 * gradient * gradient
    master = weight_old - 0.05 * (mean_next / (jnp.sqrt(square_next) + 1e-08) + 0.1 * weight_old)
    mean_scales = block_peak(jnp.abs(mean_next))
    square_scales = block_peak(square_next)
    mean_codes = (mean_next / mean_scales.astype(jnp.float32)[:, None]).astype(jnp.bfloat16)
    square_codes = (square_next / square_scales.astype(jnp.float32)[:, None]).astype(jnp.bfloat16)
    weights = lax.all_gather(master.astype(jnp.bfloat16), "dp", axis=0, tiled=True)
    return (weights, master, mean_codes, mean_scales, square_codes, square_scales)


def solution(mesh):
    in_specs = (
        P("dp", "fsdp", None),
        P(("fsdp", "dp"), None),
        P(("fsdp", "dp"), None),
        P(("fsdp", "dp")),
        P(("fsdp", "dp"), None),
        P(("fsdp", "dp")),
        P(),
    )
    out_specs = (
        P("fsdp", None),
        P(("fsdp", "dp"), None),
        P(("fsdp", "dp"), None),
        P(("fsdp", "dp")),
        P(("fsdp", "dp"), None),
        P(("fsdp", "dp")),
    )
    return jax.shard_map(local, mesh=mesh, in_specs=in_specs, out_specs=out_specs, check_vma=False)
```

profile of v0, /device:TPU:1, one launch (start us, length us, event | category | flops | bytes accessed | tf_op | source)
XLA Modules:
  0.0 145.3 jit_solution(600305273660461602)
XLA Ops:
  7.2 0.0 copy-start
  7.2 0.0 reduce-scatter.2.cloned.1.call-start
  7.2 0.0 copy-start.4
  7.2 0.0 copy-start.5
  7.2 0.0 copy-start.6
  7.3 0.7 reduce-scatter.2.cloned.1.call-update
  7.9 0.2 copy-done.4
  8.1 1.3 select_reduce_fusion
  9.5 0.2 select_reduce_fusion.1
  9.7 0.0 copy-done.5
  9.7 0.0 copy-done.6
  9.7 0.1 convolution_convert_fusion.3
  9.8 0.2 reshape.115
  10.0 0.7 copy.29
  10.7 11.5 %all-to-all-start.2 = ((bf16[128,2,2]{1,2,0:T(2,128)(2,1)}), bf16[128,2,2]{1,2,0:T(2,128)(2,1)S(1)}, u32[]{:S(2)}, u32[]{:S(2)}) async-start(bf16[128,2,2]{1,2,0:T(2,128)(2,1)} %copy.29), calls=%async_computation.2 | async-start | bytes 131072 | tf_op jit(solution)/shard_map/all_to_all | solution.py:67
  22.2 0.0 copy-done
  22.2 1.0 convolution_convert_fusion.2
  23.3 0.0 copy-start.2
  23.3 0.0 copy-start.3
  23.3 1.5 %convert_element_type.77 = bf16[128,2,2048]{2,1,0:T(2,128)(2,1)} reshape(bf16[256,2048]{1,0:T(8,128)(2,1)S(1)} %convolution_convert_fusion.2) | data formatting | bytes 2097152 | tf_op jit(solution)/shard_map/convert_element_type | solution.py:70
  24.8 6.9 %all-to-all-done.2 = bf16[128,2,2]{1,2,0:T(2,128)(2,1)S(1)} async-done(((bf16[128,2,2]{1,2,0:T(2,128)(2,1)}), bf16[128,2,2]{1,2,0:T(2,128)(2,1)S(1)}, u32[]{:S(2)}, u32[]{:S(2)}) %all-to-all-start.2) | async-done | bytes 1056 | tf_op jit(solution)/shard_map/all_to_all | solution.py:67
  31.7 5.4 %all-to-all-start = ((bf16[128,2,2048]{2,1,0:T(2,128)(2,1)}), bf16[128,2,2048]{2,1,0:T(2,128)(2,1)}, u32[]{:S(2)}, u32[]{:S(2)}) async-start(bf16[128,2,2048]{2,1,0:T(2,128)(2,1)} %convert_element_type.77), calls=%async_computation | async-start | bytes 2097152 | tf_op jit(solution)/shard_map/all_to_all | solution.py:69
  37.0 0.0 copy-done.2
  37.0 0.3 copy.25
  37.3 0.0 copy-done.3
  37.3 0.3 copy.26
  37.6 0.1 pad_maximum_fusion
  37.7 0.7 convolution_convert_fusion
  38.4 2.8 %reshape_reshape.6 = bf16[128,2,2,2048]{3,2,1,0:T(2,128)(2,1)} reshape(bf16[256,4096]{1,0:T(8,128)(2,1)S(1)} %convolution_convert_fusion) | data formatting | bytes 4194304 | tf_op jit(solution)/shard_map/reshape;reshape | solution.py:62
  41.2 14.7 %all-to-all-done = bf16[128,2,2048]{2,1,0:T(2,128)(2,1)} async-done(((bf16[128,2,2048]{2,1,0:T(2,128)(2,1)}), bf16[128,2,2048]{2,1,0:T(2,128)(2,1)}, u32[]{:S(2)}, u32[]{:S(2)}) %all-to-all-start) | async-done | bytes 1048608 | tf_op jit(solution)/shard_map/all_to_all | solution.py:69
  55.9 5.8 %all-to-all-start.1 = ((bf16[128,2,2,2048]{3,2,1,0:T(2,128)(2,1)}), bf16[128,2,2,2048]{3,2,1,0:T(2,128)(2,1)S(1)}, u32[]{:S(2)}, u32[]{:S(2)}) async-start(bf16[128,2,2,2048]{3,2,1,0:T(2,128)(2,1)} %reshape_reshape.6), calls=%async_computation.1 | async-start | bytes 4194304 | tf_op jit(solution)/shard_map/all_to_all | solution.py:66
  61.7 0.2 all-gather.2.cloned.1.call-start
  61.9 0.1 and_select_fusion.2
  62.0 0.2 select_reduce_fusion.2
  62.2 0.1 multiply_add_fusion.1
  62.3 0.1 reshape.116
  62.4 0.2 fusion.1
  62.6 2.3 %reshape.113 = bf16[256,2048]{1,0:T(8,128)(2,1)} reshape(bf16[128,2,2048]{2,1,0:T(2,128)(2,1)} %all-to-all-done) | data formatting | bytes 2097152 | tf_op jit(solution)/shard_map/reshape | solution.py:76
  64.9 27.1 %all-to-all-done.1 = bf16[128,2,2,2048]{3,2,1,0:T(2,128)(2,1)S(1)} async-done(((bf16[128,2,2,2048]{3,2,1,0:T(2,128)(2,1)}), bf16[128,2,2,2048]{3,2,1,0:T(2,128)(2,1)S(1)}, u32[]{:S(2)}, u32[]{:S(2)}) %all-to-all-start.1) | async-done | bytes 2097184 | tf_op jit(solution)/shard_map/all_to_all | solution.py:66
  92.1 0.9 copy.34
  93.0 1.8 %fusion = f32[128,4096]{1,0:T(8,128)} fusion(bf16[256,4096]{1,0:T(8,128)(2,1)S(1)} %bitcast.49, s32[128]{0:T(128)S(1)} %multiply_add_fusion.1), kind=kOutput, calls=%fused_computation.3 | convolution fusion | flops 269516800 | bytes 4194816 | tf_op jit(solution)/shard_map/dot_general | solution.py:15
  94.8 1.9 %copy.27 = f32[128,4096]{0,1:T(8,128)S(1)} copy(f32[128,4096]{1,0:T(8,128)} %fusion) | data formatting | bytes 4194304 | tf_op jit(solution)/shard_map/convert_element_type | solution.py:74
  96.7 1.5 fusion.21
  98.1 1.6 %copy.33 = f32[128,1,2048]{2,0,1:T(8,128)S(1)} copy(f32[128,1,2048]{0,2,1:T(8,128)} %get-tuple-element.12) | data formatting | bytes 2097152
  99.7 1.6 %copy.32 = f32[128,1,2048]{2,0,1:T(8,128)S(1)} copy(f32[128,1,2048]{0,2,1:T(8,128)} %get-tuple-element.13) | data formatting | bytes 2097152
  101.3 0.0 reduce-scatter.2.cloned.1.call-done
  101.3 3.5 %fusion.22 = (bf16[128,2048]{1,0:T(8,128)(2,1)}, f32[128,2048]{1,0:T(8,128)}) fusion(f32[128]{0:T(128)S(1)} %get-tuple-element.16, f32[128,1,2048]{2,0,1:T(8,128)S(1)} %copy.33, bf16[128,2048]{1,0:T(8,128)(2,1)} %reduce-scatter.2.cloned.1.call-done, f32[128]{0:T(128)S(1)} %get-tuple-element.17, f32[128,1,2048]{2,0,1:T(8,128)S(1)} %copy.32, ...), kind=kOutput, calls=%fused_computation.58 | convolution fusion | flops 138706944 | bytes 5244416 | tf_op jit(solution)/shard_map/dot_general | solution.py:20
  104.8 0.0 all-gather.2.cloned.1.call-update
  104.9 0.0 copy-start.1
  104.9 1.7 %fusion.18 = (f32[128]{0:T(128)S(1)}, f32[128]{0:T(128)S(1)}) fusion(bf16[128,2048]{1,0:T(8,128)(2,1)} %reduce-scatter.2.cloned.1.call-done, f32[128]{0:T(128)S(1)} %get-tuple-element.16, f32[128,1,2048]{2,0,1:T(8,128)S(1)} %copy.33, f32[128]{0:T(128)S(1)} %get-tuple-element.17, f32[128,1,2048]{2,0,1:T(8,128)S(1)} %copy.32), kind=kLoop, calls=%fused_computation.54 | loop fusion | flops 3407616 | bytes 2623488 | tf_op jit(solution)/shard_map/reduce_max | solution.py:29
  106.5 0.5 fusion.19
  107.1 0.0 copy-done.1
  107.1 1.4 divide_convert_fusion
  108.5 25.1 %all-gather.2.cloned.1.call-done = bf16[1024,2048]{1,0:T(8,128)(2,1)} async-done(((bf16[128,2048]{1,0:T(8,128)(2,1)}), bf16[1024,2048]{1,0:T(8,128)(2,1)}) %all-gather.2.cloned.1.call-update) | async-done | bytes 4194320 | tf_op jit(solution)/shard_map/all_gather | solution.py:86
  133.6 4.8 %copy.36 = bf16[1024,2048]{1,0:T(8,128)(2,1)} copy(bf16[1024,2048]{1,0:T(8,128)(2,1)} %all-gather.2.cloned.1.call-done) | data formatting | bytes 8388608
  (5 shorter events, 0.0 us)
Async XLA Ops:
  7.2 15.1 %copy-start = (f32[128,2048]{1,0:T(8,128)S(1)}, f32[128,2048]{1,0:T(8,128)}, u32[]{:S(2)}) copy-start(f32[128,2048]{1,0:T(8,128)} %param.8) | copy-start | bytes 3145732
  7.2 94.1 %reduce-scatter.2.cloned.1.call-start = ((), (), s32[]{:S(2)}) async-start(), calls=%async_computation.4 | async-start | bytes 4718592 | tf_op jit(solution)/shard_map/reduce_scatter | solution.py:39
  7.2 0.9 copy-start.4
  7.2 2.4 %copy-start.5 = (bf16[128]{0:T(256)(128)(2,1)S(1)}, bf16[128]{0:T(256)(128)(2,1)}, u32[]{:S(2)}) copy-start(bf16[128]{0:T(256)(128)(2,1)} %param.12) | copy-start | bytes 772
  7.2 2.4 %copy-start.6 = (bf16[128]{0:T(256)(128)(2,1)S(1)}, bf16[128]{0:T(256)(128)(2,1)}, u32[]{:S(2)}) copy-start(bf16[128]{0:T(256)(128)(2,1)} %param.10) | copy-start | bytes 772
  10.7 20.9 %all-to-all-start.2 = ((bf16[128,2,2]{1,2,0:T(2,128)(2,1)}), bf16[128,2,2]{1,2,0:T(2,128)(2,1)S(1)}, u32[]{:S(2)}, u32[]{:S(2)}) async-start(bf16[128,2,2]{1,2,0:T(2,128)(2,1)} %copy.29), calls=%async_computation.2 | async-start | bytes 131072 | tf_op jit(solution)/shard_map/all_to_all | solution.py:67
  23.3 13.8 %copy-start.2 = (bf16[128,2048]{1,0:T(8,128)(2,1)S(1)}, bf16[128,2048]{1,0:T(8,128)(2,1)}, u32[]{:S(2)}) copy-start(bf16[128,2048]{1,0:T(8,128)(2,1)} %param.9) | copy-start | bytes 1572868
  23.3 14.0 %copy-start.3 = (bf16[128,2048]{1,0:T(8,128)(2,1)S(1)}, bf16[128,2048]{1,0:T(8,128)(2,1)}, u32[]{:S(2)}) copy-start(bf16[128,2048]{1,0:T(8,128)(2,1)} %param.11) | copy-start | bytes 1572868
  31.7 24.2 %all-to-all-start = ((bf16[128,2,2048]{2,1,0:T(2,128)(2,1)}), bf16[128,2,2048]{2,1,0:T(2,128)(2,1)}, u32[]{:S(2)}, u32[]{:S(2)}) async-start(bf16[128,2,2048]{2,1,0:T(2,128)(2,1)} %convert_element_type.77), calls=%async_computation | async-start | bytes 2097152 | tf_op jit(solution)/shard_map/all_to_all | solution.py:69
  55.9 36.2 %all-to-all-start.1 = ((bf16[128,2,2,2048]{3,2,1,0:T(2,128)(2,1)}), bf16[128,2,2,2048]{3,2,1,0:T(2,128)(2,1)S(1)}, u32[]{:S(2)}, u32[]{:S(2)}) async-start(bf16[128,2,2,2048]{3,2,1,0:T(2,128)(2,1)} %reshape_reshape.6), calls=%async_computation.1 | async-start | bytes 4194304 | tf_op jit(solution)/shard_map/all_to_all | solution.py:66
  61.7 72.0 %all-gather.2.cloned.1.call-start = ((), (), s32[]{:S(2)}) async-start(), calls=%async_computation.5 | async-start | bytes 4718592 | tf_op jit(solution)/shard_map/all_gather | solution.py:86
  104.9 2.2 %copy-start.1 = (bf16[128,2048]{1,0:T(8,128)(2,1)S(1)}, bf16[128,2048]{1,0:T(8,128)(2,1)}, u32[]{:S(2)}) copy-start(bf16[128,2048]{1,0:T(8,128)(2,1)} %reduce-scatter.2.cloned.1.call-done) | copy-start | bytes 1572868
Sparse Core Ops, SparseCore 0:
  10.4 50.0 reduce-scatter.1
  105.0 28.6 all-gather.1
where the time goes:
time: 146 us; the launch traced here: 145 us
  waiting for transfers between devices  74.5 us (51%)
  starting transfers between devices  22.9 us (16%)
  local copies, waits for them, and re-layouts  20.5 us (14%)
  between operations  14.3 us (10%)
  matrix products  7.42 us (5%)
  other arithmetic  5.6 us (4%)
    all_to_all x1, waiting for transfers between devices, local(): lax.all_to_all(code_buffer, ('fsdp', 'dp'), split_axis=0, concat_axis=0,...  27.1 us
    all_gather x1, waiting for transfers between devices, local(): lax.all_gather(master.astype(jnp.bfloat16), 'dp', axis=0, tiled=True)  25.1 us
    all_to_all x1, waiting for transfers between devices, local(): lax.all_to_all(master_buffer.astype(jnp.bfloat16), ('fsdp', 'dp'), split_...  14.7 us
    all_to_all x1, starting transfers between devices, local(): lax.all_to_all(scale_buffer, ('fsdp', 'dp'), split_axis=0, concat_axis=0,...  11.5 us
    unnamed x20, local copies, waits for them, and re-layouts  9.58 us
    all_to_all x1, waiting for transfers between devices, local(): lax.all_to_all(scale_buffer, ('fsdp', 'dp'), split_axis=0, concat_axis=0,...  6.87 us
    all_to_all x1, starting transfers between devices, local(): lax.all_to_all(code_buffer, ('fsdp', 'dp'), split_axis=0, concat_axis=0,...  5.78 us
    all_to_all x1, starting transfers between devices, local(): lax.all_to_all(master_buffer.astype(jnp.bfloat16), ('fsdp', 'dp'), split_...  5.36 us
  transfers between devices with their start and end apart: 5, of which 4 were waited for; matrix products, arithmetic and copies ran while one was open for 17% of the time, Pallas kernels for 0%

commit v1 on v0

--- a/solution.py
+++ b/solution.py
@@ -83,7 +83,11 @@
     square_scales = block_peak(square_next)
     mean_codes = (mean_next / mean_scales.astype(jnp.float32)[:, None]).astype(jnp.bfloat16)
     square_codes = (square_next / square_scales.astype(jnp.float32)[:, None]).astype(jnp.bfloat16)
-    weights = lax.all_gather(master.astype(jnp.bfloat16), "dp", axis=0, tiled=True)
+    own = master.astype(jnp.bfloat16)
+    peers = lax.axis_size("dp")
+    blocks = jnp.stack([own for _ in range(peers)])
+    blocks = lax.all_to_all(blocks, "dp", split_axis=0, concat_axis=0)
+    weights = jnp.concatenate(blocks, axis=0)
     return (weights, master, mean_codes, mean_scales, square_codes, square_scales)
 
 

time: 146 us -> 174 us (1.19)
  waiting for transfers between devices: 74.5 us -> 94.9 us
  starting transfers between devices: 22.9 us -> 28.2 us
  local copies, waits for them, and re-layouts: 20.5 us -> 23.1 us
    all_to_all x0 -> x1, waiting for transfers between devices: none -> 45.3 us  [local(): blocks = lax.all_to_all(blocks, 'dp', split_axis=0, concat_axis=0)]
    all_gather x1 -> x0, waiting for transfers between devices: 25.1 us -> none  [local(): lax.all_gather(master.astype(jnp.bfloat16), 'dp', axis=0, tiled=True)]
    all_to_all x0 -> x1, starting transfers between devices: none -> 5.53 us  [local(): blocks = lax.all_to_all(blocks, 'dp', split_axis=0, concat_axis=0)]
    another operation x0 -> x1, local copies, waits for them, and re-layouts: none -> 2.54 us  [local(): blocks = jnp.stack([own for _ in range(peers)])]
  transfers between devices with their start and end apart: 5 -> 5, of which waited for: 4 -> 4; matrix products, arithmetic and copies ran while one was open for 17% -> 14% of each run, Pallas kernels for 0% -> 0%
where the time goes in v1:
time: 174 us; the launch traced here: 173 us
  waiting for transfers between devices  94.9 us (55%)
  starting transfers between devices  28.2 us (16%)
  local copies, waits for them, and re-layouts  23.1 us (13%)
  between operations  14.3 us (8%)
  matrix products  7.25 us (4%)
  other arithmetic  5.6 us (3%)
    all_to_all x1, waiting for transfers between devices, local(): blocks = lax.all_to_all(blocks, 'dp', split_axis=0, concat_axis=0)  45.3 us
    all_to_all x1, waiting for transfers between devices, local(): lax.all_to_all(code_buffer, ('fsdp', 'dp'), split_axis=0, concat_axis=0,...  27.4 us
    all_to_all x1, waiting for transfers between devices, local(): lax.all_to_all(master_buffer.astype(jnp.bfloat16), ('fsdp', 'dp'), split_...  14.7 us
    all_to_all x1, starting transfers between devices, local(): lax.all_to_all(scale_buffer, ('fsdp', 'dp'), split_axis=0, concat_axis=0,...  11.5 us
    unnamed x20, local copies, waits for them, and re-layouts  9.58 us
    all_to_all x1, waiting for transfers between devices, local(): lax.all_to_all(scale_buffer, ('fsdp', 'dp'), split_axis=0, concat_axis=0,...  6.87 us
    all_to_all x1, starting transfers between devices, local(): lax.all_to_all(code_buffer, ('fsdp', 'dp'), split_axis=0, concat_axis=0,...  5.78 us
    all_to_all x1, starting transfers between devices, local(): blocks = lax.all_to_all(blocks, 'dp', split_axis=0, concat_axis=0)  5.53 us
  transfers between devices with their start and end apart: 5, of which 4 were waited for; matrix products, arithmetic and copies ran while one was open for 14% of the time, Pallas kernels for 0%

profile of v1, /device:TPU:1, one launch (start us, length us, event | category | flops | bytes accessed | tf_op | source)
XLA Modules:
  0.0 173.3 jit_solution(10838769354415888807)
XLA Ops:
  7.2 0.0 copy-start
  7.2 0.0 reduce-scatter.2.cloned.1.call-start
  7.2 0.0 copy-start.4
  7.2 0.0 copy-start.5
  7.2 0.0 copy-start.6
  7.3 0.7 reduce-scatter.2.cloned.1.call-update
  7.9 0.2 copy-done.4
  8.1 1.3 select_reduce_fusion
  9.5 0.2 select_reduce_fusion.1
  9.7 0.0 copy-done.5
  9.7 0.0 copy-done.6
  9.7 0.1 convolution_convert_fusion.3
  9.8 0.2 reshape.120
  10.0 0.7 copy.29
  10.7 11.5 %all-to-all-start.2 = ((bf16[128,2,2]{1,2,0:T(2,128)(2,1)}), bf16[128,2,2]{1,2,0:T(2,128)(2,1)S(1)}, u32[]{:S(2)}, u32[]{:S(2)}) async-start(bf16[128,2,2]{1,2,0:T(2,128)(2,1)} %copy.29), calls=%async_computation.2 | async-start | bytes 131072 | tf_op jit(solution)/shard_map/all_to_all | solution.py:67
  22.2 0.0 copy-done
  22.2 1.0 convolution_convert_fusion.2
  23.3 0.0 copy-start.2
  23.3 0.0 copy-start.3
  23.3 1.5 convert_element_type.77
  24.8 6.9 %all-to-all-done.2 = bf16[128,2,2]{1,2,0:T(2,128)(2,1)S(1)} async-done(((bf16[128,2,2]{1,2,0:T(2,128)(2,1)}), bf16[128,2,2]{1,2,0:T(2,128)(2,1)S(1)}, u32[]{:S(2)}, u32[]{:S(2)}) %all-to-all-start.2) | async-done | bytes 1056 | tf_op jit(solution)/shard_map/all_to_all | solution.py:67
  31.7 5.4 %all-to-all-start = ((bf16[128,2,2048]{2,1,0:T(2,128)(2,1)}), bf16[128,2,2048]{2,1,0:T(2,128)(2,1)}, u32[]{:S(2)}, u32[]{:S(2)}) async-start(bf16[128,2,2048]{2,1,0:T(2,128)(2,1)} %convert_element_type.77), calls=%async_computation | async-start | bytes 2097152 | tf_op jit(solution)/shard_map/all_to_all | solution.py:69
  37.0 0.0 copy-done.2
  37.0 0.3 copy.25
  37.3 0.0 copy-done.3
  37.3 0.3 copy.26
  37.6 0.1 pad_maximum_fusion
  37.7 0.7 convolution_convert_fusion
  38.4 2.8 %reshape_reshape.6 = bf16[128,2,2,2048]{3,2,1,0:T(2,128)(2,1)} reshape(bf16[256,4096]{1,0:T(8,128)(2,1)S(1)} %convolution_convert_fusion) | data formatting | bytes 4194304 | tf_op jit(solution)/shard_map/reshape;reshape | solution.py:62
  41.2 14.7 %all-to-all-done = bf16[128,2,2048]{2,1,0:T(2,128)(2,1)} async-done(((bf16[128,2,2048]{2,1,0:T(2,128)(2,1)}), bf16[128,2,2048]{2,1,0:T(2,128)(2,1)}, u32[]{:S(2)}, u32[]{:S(2)}) %all-to-all-start) | async-done | bytes 1048608 | tf_op jit(solution)/shard_map/all_to_all | solution.py:69
  55.9 5.8 %all-to-all-start.1 = ((bf16[128,2,2,2048]{3,2,1,0:T(2,128)(2,1)}), bf16[128,2,2,2048]{3,2,1,0:T(2,128)(2,1)S(1)}, u32[]{:S(2)}, u32[]{:S(2)}) async-start(bf16[128,2,2,2048]{3,2,1,0:T(2,128)(2,1)} %reshape_reshape.6), calls=%async_computation.1 | async-start | bytes 4194304 | tf_op jit(solution)/shard_map/all_to_all | solution.py:66
  61.7 0.1 and_select_fusion.2
  61.8 0.2 select_reduce_fusion.2
  61.9 0.1 multiply_add_fusion.1
  62.1 0.1 reshape.121
  62.2 0.2 fusion.1
  62.4 2.3 %reshape.118 = bf16[256,2048]{1,0:T(8,128)(2,1)} reshape(bf16[128,2,2048]{2,1,0:T(2,128)(2,1)} %all-to-all-done) | data formatting | bytes 2097152 | tf_op jit(solution)/shard_map/reshape | solution.py:76
  64.7 27.4 %all-to-all-done.1 = bf16[128,2,2,2048]{3,2,1,0:T(2,128)(2,1)S(1)} async-done(((bf16[128,2,2,2048]{3,2,1,0:T(2,128)(2,1)}), bf16[128,2,2,2048]{3,2,1,0:T(2,128)(2,1)S(1)}, u32[]{:S(2)}, u32[]{:S(2)}) %all-to-all-start.1) | async-done | bytes 2097184 | tf_op jit(solution)/shard_map/all_to_all | solution.py:66
  92.1 0.9 copy.34
  93.0 1.8 %fusion = f32[128,4096]{1,0:T(8,128)} fusion(bf16[256,4096]{1,0:T(8,128)(2,1)S(1)} %bitcast.50, s32[128]{0:T(128)S(1)} %multiply_add_fusion.1), kind=kOutput, calls=%fused_computation.3 | convolution fusion | flops 269516800 | bytes 4194816 | tf_op jit(solution)/shard_map/dot_general | solution.py:15
  94.8 1.9 %copy.27 = f32[128,4096]{0,1:T(8,128)S(1)} copy(f32[128,4096]{1,0:T(8,128)} %fusion) | data formatting | bytes 4194304 | tf_op jit(solution)/shard_map/convert_element_type | solution.py:74
  96.7 1.5 fusion.21
  98.1 1.6 copy.33
  99.7 1.6 copy.32
  101.3 0.0 reduce-scatter.2.cloned.1.call-done
  101.3 3.4 %fusion.22 = (bf16[128,2048]{1,0:T(8,128)(2,1)S(1)}, f32[128,2048]{1,0:T(8,128)}) fusion(f32[128]{0:T(128)S(1)} %get-tuple-element.16, f32[128,1,2048]{2,0,1:T(8,128)S(1)} %copy.33, bf16[128,2048]{1,0:T(8,128)(2,1)} %reduce-scatter.2.cloned.1.call-done, f32[128]{0:T(128)S(1)} %get-tuple-element.17, f32[128,1,2048]{2,0,1:T(8,128)S(1)} %copy.32, ...), kind=kOutput, calls=%fused_computation.58 | convolution fusion | flops 138706944 | bytes 5244416 | tf_op jit(solution)/shard_map/dot_general | solution.py:20
  104.7 2.5 %stack.35 = bf16[8,128,2048]{2,1,0:T(8,128)(2,1)} broadcast(bf16[128,2048]{1,0:T(8,128)(2,1)S(1)} %get-tuple-element.20), dimensions={1,2} | broadcast | bytes 4718592 | tf_op jit(solution)/shard_map/stack | solution.py:88
  107.2 5.5 %all-to-all-start.3 = ((bf16[8,128,2048]{2,1,0:T(8,128)(2,1)}), bf16[8,128,2048]{2,1,0:T(8,128)(2,1)}, u32[]{:S(2)}, u32[]{:S(2)}) async-start(bf16[8,128,2048]{2,1,0:T(8,128)(2,1)} %stack.35), calls=%async_computation.4 | async-start | bytes 8388608 | tf_op jit(solution)/shard_map/all_to_all | solution.py:89
  112.7 0.0 copy-start.1
  112.7 1.7 fusion.18
  114.4 0.5 fusion.19
  114.9 0.0 copy-done.1
  114.9 1.4 divide_convert_fusion
  116.4 45.3 %all-to-all-done.3 = bf16[8,128,2048]{2,1,0:T(8,128)(2,1)} async-done(((bf16[8,128,2048]{2,1,0:T(8,128)(2,1)}), bf16[8,128,2048]{2,1,0:T(8,128)(2,1)}, u32[]{:S(2)}, u32[]{:S(2)}) %all-to-all-start.3) | async-done | bytes 4194336 | tf_op jit(solution)/shard_map/all_to_all | solution.py:89
  161.7 4.8 %copy.36 = bf16[1024,2048]{1,0:T(8,128)(2,1)} copy(bf16[1024,2048]{1,0:T(8,128)(2,1)} %bitcast.11) | data formatting | bytes 8388608
  (5 shorter events, 0.0 us)
Async XLA Ops:
  7.2 15.1 %copy-start = (f32[128,2048]{1,0:T(8,128)S(1)}, f32[128,2048]{1,0:T(8,128)}, u32[]{:S(2)}) copy-start(f32[128,2048]{1,0:T(8,128)} %param.8) | copy-start | bytes 3145732
  7.2 94.1 %reduce-scatter.2.cloned.1.call-start = ((), (), s32[]{:S(2)}) async-start(), calls=%async_computation.5 | async-start | bytes 4718592 | tf_op jit(solution)/shard_map/reduce_scatter | solution.py:39
  7.2 0.9 copy-start.4
  7.2 2.4 %copy-start.5 = (bf16[128]{0:T(256)(128)(2,1)S(1)}, bf16[128]{0:T(256)(128)(2,1)}, u32[]{:S(2)}) copy-start(bf16[128]{0:T(256)(128)(2,1)} %param.12) | copy-start | bytes 772
  7.2 2.4 %copy-start.6 = (bf16[128]{0:T(256)(128)(2,1)S(1)}, bf16[128]{0:T(256)(128)(2,1)}, u32[]{:S(2)}) copy-start(bf16[128]{0:T(256)(128)(2,1)} %param.10) | copy-start | bytes 772
  10.7 20.9 %all-to-all-start.2 = ((bf16[128,2,2]{1,2,0:T(2,128)(2,1)}), bf16[128,2,2]{1,2,0:T(2,128)(2,1)S(1)}, u32[]{:S(2)}, u32[]{:S(2)}) async-start(bf16[128,2,2]{1,2,0:T(2,128)(2,1)} %copy.29), calls=%async_computation.2 | async-start | bytes 131072 | tf_op jit(solution)/shard_map/all_to_all | solution.py:67
  23.3 13.8 %copy-start.2 = (bf16[128,2048]{1,0:T(8,128)(2,1)S(1)}, bf16[128,2048]{1,0:T(8,128)(2,1)}, u32[]{:S(2)}) copy-start(bf16[128,2048]{1,0:T(8,128)(2,1)} %param.9) | copy-start | bytes 1572868
  23.3 14.0 %copy-start.3 = (bf16[128,2048]{1,0:T(8,128)(2,1)S(1)}, bf16[128,2048]{1,0:T(8,128)(2,1)}, u32[]{:S(2)}) copy-start(bf16[128,2048]{1,0:T(8,128)(2,1)} %param.11) | copy-start | bytes 1572868
  31.7 24.2 %all-to-all-start = ((bf16[128,2,2048]{2,1,0:T(2,128)(2,1)}), bf16[128,2,2048]{2,1,0:T(2,128)(2,1)}, u32[]{:S(2)}, u32[]{:S(2)}) async-start(bf16[128,2,2048]{2,1,0:T(2,128)(2,1)} %convert_element_type.77), calls=%async_computation | async-start | bytes 2097152 | tf_op jit(solution)/shard_map/all_to_all | solution.py:69
  55.9 36.2 %all-to-all-start.1 = ((bf16[128,2,2,2048]{3,2,1,0:T(2,128)(2,1)}), bf16[128,2,2,2048]{3,2,1,0:T(2,128)(2,1)S(1)}, u32[]{:S(2)}, u32[]{:S(2)}) async-start(bf16[128,2,2,2048]{3,2,1,0:T(2,128)(2,1)} %reshape_reshape.6), calls=%async_computation.1 | async-start | bytes 4194304 | tf_op jit(solution)/shard_map/all_to_all | solution.py:66
  107.2 54.5 %all-to-all-start.3 = ((bf16[8,128,2048]{2,1,0:T(8,128)(2,1)}), bf16[8,128,2048]{2,1,0:T(8,128)(2,1)}, u32[]{:S(2)}, u32[]{:S(2)}) async-start(bf16[8,128,2048]{2,1,0:T(8,128)(2,1)} %stack.35), calls=%async_computation.4 | async-start | bytes 8388608 | tf_op jit(solution)/shard_map/all_to_all | solution.py:89
  112.7 2.2 %copy-start.1 = (bf16[128,2048]{1,0:T(8,128)(2,1)S(1)}, bf16[128,2048]{1,0:T(8,128)(2,1)}, u32[]{:S(2)}) copy-start(bf16[128,2048]{1,0:T(8,128)(2,1)} %reduce-scatter.2.cloned.1.call-done) | copy-start | bytes 1572868
Sparse Core Ops, SparseCore 0:
  10.4 50.0 reduce-scatter.1
